TPU v7x, 32 devices: a whole 2x2x4 slice. The times are simulated.
32 devices in a mesh: grp: 2 (over y), tile: 4 (over z), span: 4 (over x, core).
Axes of the slice: x: 2, y: 2, z: 4, core: 2. Of those that a mesh axis runs over, the one named last changes fastest.
Arguments:
- features: bfloat16 [16, 8, 160, 384], P(('grp', 'span'), 'tile'), parts along dimension 0, may hold values from -24 to 24
- clip_lengths: int32 [8], P('grp'), parts along dimension 0, may hold values from 1 to 4, as said below
- norm_gain: float32 [384], replicated, may hold values from 0.1 to 1.9
- w_qkv: bfloat16 [384, 1152], replicated, may hold values from -6 to 6
- w_out: bfloat16 [384, 384], replicated, may hold values from -1 to 1
- conv_gain: float32 [384], replicated, may hold values from 0.1 to 1.9
- w_conv: bfloat16 [3, 3, 3, 384, 384], replicated, may hold values from -0.0625 to 0.0625
Outputs:
- attended: bfloat16 [16, 8, 160, 384], P(('grp', 'span'), 'tile'), parts along dimension 0
- hidden: bfloat16 [16, 8, 160, 384], P(('grp', 'span'), 'tile'), parts along dimension 0
There are 2 independent parts, one for each index of `grp`. A program takes and returns all parts, laid end to end along the dimension named above; an argument that names none is the same for every part. Nothing has to cross between parts.
Inputs may be any that keep to these rules, and one draw needn't show every extreme that they name: `clip_lengths`: the lengths sum to 8; exactly one clip has 4 frames.
All inputs are finite; a program needn't handle non-finite values.
Results may differ from a plain program's by a relative error of at most 0.0095.
The roundings to bfloat16 on the way count: a program that leaves them out, or rounds other values in their place, can miss the bound.
Values may be sent and summed in bfloat16 or wider, within the bound.
No kernel may reach another device: no remote copies, remote signals or barrier semaphores. Data moves between devices by JAX's collectives and lax.ppermute only.
A program may use at most 128 MiB of HBM per device.

v0:
```python
import jax
import jax.numpy as jnp
from jax import lax
from jax.sharding import PartitionSpec as P

eps = 1e-06


def from_behind(block, axis, distance):
    devices = range(lax.axis_size(axis))
    route = [(i - distance, i) for i in devices if i - distance in devices]
    return lax.ppermute(block, axis, route)


def extended(x, sides, width):
    for axis, dim in sides:
        size, length = (lax.axis_size(axis), x.shape[dim])
        up = [(i, (i + 1) % size) for i in range(size - 1)]
        down = [(j, i) for i, j in up]
        last = lax.slice_in_dim(x, length - width, length, axis=dim)
        first = lax.slice_in_dim(x, 0, width, axis=dim)
        before = lax.ppermute(last, axis, up)
        after = lax.ppermute(first, axis, down)
        x = jnp.concatenate([before, x, after], axis=dim)
    return x


def rms_scale(values, gain_vec):
    as_float = values.astype(jnp.float32)
    return (
        as_float * lax.rsqrt(jnp.mean(as_float * as_float, axis=-1, keepdims=True) + eps) * gain_vec
    )


def on_device(features, clip_lengths, norm_gain, w_qkv, w_out, conv_gain, w_conv):
    frames, row_count, col_count, channels = features.shape
    cell_count = row_count * col_count
    normed_grid = rms_scale(features, norm_gain).astype(jnp.bfloat16)
    view_frames = normed_grid.shape[0]
    view_cells = normed_grid.shape[1] * normed_grid.shape[2]
    normed = normed_grid.reshape(view_frames, view_cells, channels)
    queries = jnp.dot(
        normed.reshape(-1, channels), w_qkv[:, :channels], preferred_element_type=jnp.float32
    )
    queries = queries.astype(jnp.bfloat16).reshape(view_frames, view_cells, channels)
    kv_weight = w_qkv[:, channels:]
    score_scale = channels ** (-0.5)
    outgoing = jnp.dot(normed.reshape(-1, channels), kv_weight, preferred_element_type=jnp.float32)
    outgoing = outgoing.astype(jnp.bfloat16).reshape(view_frames, view_cells, 2 * channels)
    portion = lax.all_gather(outgoing, "tile", axis=1, tiled=True)
    key_part = portion[:, :, :channels]
    value_part = portion[:, :, channels:]
    row_top = jnp.full((view_frames, view_cells, 1), -1e30, jnp.float32)
    scores = (
        jnp.einsum("fqc,fkc->fqk", queries, key_part, preferred_element_type=jnp.float32)
        * score_scale
    )
    new_top = jnp.maximum(row_top, jnp.max(scores, axis=2, keepdims=True))
    raised_f = jnp.exp(scores - new_top)
    row_total = jnp.sum(raised_f, axis=2, keepdims=True)
    weighted = jnp.einsum(
        "fqk,fkc->fqc",
        raised_f.astype(jnp.bfloat16),
        value_part,
        preferred_element_type=jnp.float32,
    )
    mixture_grid = (weighted / row_total).astype(jnp.bfloat16)
    mixture = mixture_grid.reshape(-1, channels)
    projected = jnp.dot(mixture, w_out, preferred_element_type=jnp.float32)
    attended = (features.reshape(-1, channels).astype(jnp.float32) + projected).astype(jnp.bfloat16)
    attended = attended.reshape(frames, row_count, col_count, channels)
    lifted = rms_scale(attended, conv_gain)
    activated = (lifted * jax.nn.sigmoid(lifted)).astype(jnp.bfloat16)
    earlier = from_behind(activated, "span", 1)
    stacked = jnp.concatenate([earlier, activated], axis=0)
    edged = extended(stacked, (("tile", 1),), 1)
    padded = jnp.pad(edged, ((0, 0), (0, 0), (1, 1), (0, 0)))
    clip_ends = jnp.cumsum(clip_lengths)
    position = lax.axis_index("span") * frames + jnp.arange(frames, dtype=jnp.int32)
    clip_start = jnp.sum(
        jnp.where(clip_ends[None, :] <= position[:, None], clip_lengths[None, :], 0), axis=1
    )
    summed = jnp.zeros((frames * cell_count, channels), jnp.float32)
    for t_tap in range(3):
        usable = position - (2 - t_tap) >= clip_start
        for r_tap in range(3):
            for c_tap in range(3):
                shifted = padded[
                    t_tap : t_tap + frames, r_tap : r_tap + row_count, c_tap : c_tap + col_count
                ]
                shifted = jnp.where(
                    usable[:, None, None, None], shifted, jnp.zeros((), shifted.dtype)
                )
                summed = summed + jnp.dot(
                    shifted.reshape(-1, channels),
                    w_conv[t_tap, r_tap, c_tap],
                    preferred_element_type=jnp.float32,
                )
    hidden = summed.astype(jnp.bfloat16).reshape(frames, row_count, col_count, channels)
    return (attended, hidden)


def solution(mesh):
    in_specs = (P(("grp", "span"), "tile", None, None), P("grp"), P(), P(), P(), P(), P())
    out_specs = (P(("grp", "span"), "tile", None, None), P(("grp", "span"), "tile", None, None))
    return jax.shard_map(
        on_device, mesh=mesh, in_specs=in_specs, out_specs=out_specs, check_vma=False
    )
```

profile of v0, /device:TPU:10, one launch (start us, length us, event | category | flops | bytes accessed | tf_op | source)
XLA Modules:
  0.0 146.0 jit_solution(7980055820085720016)
XLA Ops:
  7.2 1.3 multiply_reduce_fusion
  8.5 1.2 multiply_convert_fusion.1
  9.8 2.7 %convolution_convert_fusion = bf16[640,768]{1,0:T(8,128)(2,1)} fusion(bf16[640,384]{1,0:T(8,128)(2,1)S(1)} %bitcast.177, bf16[384,1152]{1,0:T(8,128)(2,1)} %param.10), kind=kOutput, calls=%fused_computation.18 | convolution fusion | flops 377978880 | bytes 2064384 | tf_op jit(solution)/shard_map/dot_general | solution.py:48
  12.5 1.4 convolution_convert_fusion.1
  13.9 73.9 %all-gather.2.cloned.1.call-done = bf16[2,1280,768]{2,1,0:T(8,128)(2,1)} async-done(((bf16[2,320,768]{2,1,0:T(8,128)(2,1)}), bf16[2,1280,768]{2,1,0:T(8,128)(2,1)}) %all-gather.2.cloned.1.call-update) | async-done | bytes 3932176 | tf_op jit(solution)/shard_map/all_gather | solution.py:50
  87.8 2.8 %fusion.98 = (f32[2,320]{1,0:T(2,128)S(1)}, f32[2,320,1280]{2,1,0:T(8,128)S(1)}) fusion(bf16[2,320,384]{2,1,0:T(8,128)(2,1)S(1)} %bitcast.179, bf16[2,1280,768]{2,1,0:T(8,128)(2,1)} %all-gather.2.cloned.1.call-done), kind=kOutput, calls=%fused_computation.171 | convolution fusion | flops 630783360 | bytes 5736960 | tf_op jit(solution)/shard_map/fqc,fkc->fqk/dot_general | solution.py:55
  90.6 0.6 fusion.1
  91.3 1.1 divide_convert_fusion
  92.4 0.6 fusion.14
  93.5 1.9 %collective-permute-start = (bf16[2,2,160,384]{3,2,1,0:T(8,128)(2,1)S(1)}, bf16[2,2,160,384]{3,2,1,0:T(8,128)(2,1)S(1)}, u32[]{:S(2)}, u32[]{:S(2)}) collective-permute-start(bf16[2,2,160,384]{3,2,1,0:T(8,128)(2,1)S(1)} %multiply_convert_fusion), channel_id=1, source_target_pairs={{0,1},{1,2},{2,3},{4,5},{5,6},{6,7},{8,9},{9,10},{10,11},{12,13},{... | collective-permute-start | bytes 1474568 | tf_op jit(solution)/shard_map/ppermute | solution.py:12
  95.4 8.2 %collective-permute-done = bf16[2,2,160,384]{3,2,1,0:T(8,128)(2,1)S(1)} collective-permute-done((bf16[2,2,160,384]{3,2,1,0:T(8,128)(2,1)S(1)}, bf16[2,2,160,384]{3,2,1,0:T(8,128)(2,1)S(1)}, u32[]{:S(2)}, u32[]{:S(2)}) %collective-permute-start) | collective-permute-done | bytes 491552 | tf_op jit(solution)/shard_map/ppermute | solution.py:12
  103.6 0.9 fusion.30
  104.5 4.4 %collective-permute-start.1 = (bf16[4,1,160,384]{3,2,1,0:T(8,128)(2,1)}, bf16[4,1,160,384]{3,2,1,0:T(8,128)(2,1)S(1)}, u32[]{:S(2)}, u32[]{:S(2)}) collective-permute-start(bf16[4,1,160,384]{3,2,1,0:T(8,128)(2,1)} %get-tuple-element.34), channel_id=1, source_target_pairs={{0,4},{4,8},{8,12},{1,5},{5,9},{9,13},{2,6},{6,10},{10,14},{3,7},{... | collective-permute-start | bytes 1474568 | tf_op jit(solution)/shard_map/ppermute | solution.py:22
  108.9 1.9 %collective-permute-start.2 = (bf16[4,1,160,384]{3,2,1,0:T(8,128)(2,1)S(1)}, bf16[4,1,160,384]{3,2,1,0:T(8,128)(2,1)S(1)}, u32[]{:S(2)}, u32[]{:S(2)}) collective-permute-start(bf16[4,1,160,384]{3,2,1,0:T(8,128)(2,1)S(1)} %get-tuple-element.35), channel_id=1, source_target_pairs={{4,0},{8,4},{12,8},{5,1},{9,5},{13,9},{6,2},{10,6},{14,10},{7,3},{... | collective-permute-start | bytes 1474568 | tf_op jit(solution)/shard_map/ppermute | solution.py:23
  111.4 4.4 %collective-permute-done.1 = bf16[4,1,160,384]{3,2,1,0:T(8,128)(2,1)S(1)} collective-permute-done((bf16[4,1,160,384]{3,2,1,0:T(8,128)(2,1)}, bf16[4,1,160,384]{3,2,1,0:T(8,128)(2,1)S(1)}, u32[]{:S(2)}, u32[]{:S(2)}) %collective-permute-start.1) | collective-permute-done | bytes 491552 | tf_op jit(solution)/shard_map/ppermute | solution.py:22
  115.8 3.9 %collective-permute-done.2 = bf16[4,1,160,384]{3,2,1,0:T(8,128)(2,1)S(1)} collective-permute-done((bf16[4,1,160,384]{3,2,1,0:T(8,128)(2,1)S(1)}, bf16[4,1,160,384]{3,2,1,0:T(8,128)(2,1)S(1)}, u32[]{:S(2)}, u32[]{:S(2)}) %collective-permute-start.2) | collective-permute-done | bytes 491552 | tf_op jit(solution)/shard_map/ppermute | solution.py:23
  119.6 1.2 select_maximum_fusion
  120.8 1.4 slice_select_fusion
  122.5 1.5 %slice_select_fusion.6 = (bf16[2,2,160,384]{3,2,1,0:T(8,128)(2,1)S(1)}, bf16[2,2,160,384]{3,2,1,0:T(8,128)(2,1)S(1)}, bf16[2,2,160,384]{3,2,1,0:T(8,128)(2,1)S(1...) fusion(bf16[4,3,160,384]{3,2,1,0:T(8,128)(2,1)S(1)} %get-tuple-, ...), kind=kLoop, calls=%fused_computation.77 | loop fusion | flops 3686400 | bytes 13762566 | tf_op jit(solution)/shard_map/jit(_where)/select_n | solution.py:91
  124.3 1.3 slice-done.1
  126.5 0.5 convolution_add_fusion.24
  127.0 0.5 convolution_add_fusion.23
  127.5 0.5 convolution_add_fusion.22
  128.0 0.5 fusion.11
  128.4 0.5 convolution_add_fusion.20
  129.8 0.5 convolution_add_fusion.17
  130.3 0.5 convolution_add_fusion.16
  131.7 0.5 convolution_add_fusion.13
  132.1 0.5 convolution_add_fusion.12
  135.8 0.6 convolution_add_fusion.4
  136.5 0.5 convolution_add_fusion.3
  137.9 1.2 fusion.13
  (45 shorter events, 8.4 us)
Async XLA Ops:
  7.2 85.3 %copy-start = (bf16[384,384]{1,0:T(8,128)(2,1)S(1)}, bf16[384,384]{1,0:T(8,128)(2,1)}, u32[]{:S(2)}) copy-start(bf16[384,384]{1,0:T(8,128)(2,1)} %param.11) | copy-start | bytes 884740
  7.2 80.6 %all-gather.2.cloned.1.call-start = ((), (), s32[]{:S(2)}) async-start(), calls=%async_computation | async-start | bytes 4915200 | tf_op jit(solution)/shard_map/all_gather | solution.py:50
  87.8 3.5 %copy-start.2 = (bf16[2,1280,768]{2,1,0:T(8,128)(2,1)S(1)}, bf16[2,1280,768]{2,1,0:T(8,128)(2,1)}, u32[]{:S(2)}) copy-start(bf16[2,1280,768]{2,1,0:T(8,128)(2,1)} %all-gather.2.cloned.1.call-done) | copy-start | bytes 11796484
  91.3 1.1 copy-start.1
  91.3 1.8 %copy-start.4 = (f32[384]{0:T(512)S(1)}, f32[384]{0:T(512)}, u32[]{:S(2)}) copy-start(f32[384]{0:T(512)} %param.12) | copy-start | bytes 4612
  92.4 18.4 %copy-start.5 = (s32[4]{0:T(128)S(1)}, s32[4]{0:T(128)}, u32[]{:S(2)}) copy-start(s32[4]{0:T(128)} %param.8) | copy-start | bytes 52
  93.0 42.8 %copy-start.3 = (bf16[640,384]{1,0:T(8,128)(2,1)}, bf16[640,384]{1,0:T(8,128)(2,1)S(1)}, u32[]{:S(2)}) copy-start(bf16[640,384]{1,0:T(8,128)(2,1)S(1)} %get-tuple-element.55) | copy-start | bytes 1474564
  93.5 10.1 %collective-permute-start = (bf16[2,2,160,384]{3,2,1,0:T(8,128)(2,1)S(1)}, bf16[2,2,160,384]{3,2,1,0:T(8,128)(2,1)S(1)}, u32[]{:S(2)}, u32[]{:S(2)}) collective-permute-start(bf16[2,2,160,384]{3,2,1,0:T(8,128)(2,1)S(1)} %multiply_convert_fusion), channel_id=1, source_target_pairs={{0,1},{1,2},{2,3},{4,5},{5,6},{6,7},{8,9},{9,10},{10,11},{12,13},{... | collective-permute-start | bytes 1474568 | tf_op jit(solution)/shard_map/ppermute | solution.py:12
  104.5 11.2 %collective-permute-start.1 = (bf16[4,1,160,384]{3,2,1,0:T(8,128)(2,1)}, bf16[4,1,160,384]{3,2,1,0:T(8,128)(2,1)S(1)}, u32[]{:S(2)}, u32[]{:S(2)}) collective-permute-start(bf16[4,1,160,384]{3,2,1,0:T(8,128)(2,1)} %get-tuple-element.34), channel_id=1, source_target_pairs={{0,4},{4,8},{8,12},{1,5},{5,9},{9,13},{2,6},{6,10},{10,14},{3,7},{... | collective-permute-start | bytes 1474568 | tf_op jit(solution)/shard_map/ppermute | solution.py:22
  108.9 10.7 %collective-permute-start.2 = (bf16[4,1,160,384]{3,2,1,0:T(8,128)(2,1)S(1)}, bf16[4,1,160,384]{3,2,1,0:T(8,128)(2,1)S(1)}, u32[]{:S(2)}, u32[]{:S(2)}) collective-permute-start(bf16[4,1,160,384]{3,2,1,0:T(8,128)(2,1)S(1)} %get-tuple-element.35), channel_id=1, source_target_pairs={{4,0},{8,4},{12,8},{5,1},{9,5},{13,9},{6,2},{10,6},{14,10},{7,3},{... | collective-permute-start | bytes 1474568 | tf_op jit(solution)/shard_map/ppermute | solution.py:23
  122.2 2.1 %slice-start = ((s8[7962624]{0:T(1024)(128)(4,1)}), s8[3768320]{0:T(1024)(128)(4,1)S(1)}, s32[]{:S(2)}) async-start(s8[7962624]{0:T(1024)(128)(4,1)} %bitcast.148), calls=%async_computation.1 | async-start | bytes 7536640
  122.5 3.1 %slice-start.1 = ((s8[7962624]{0:T(1024)(128)(4,1)}), s8[4194304]{0:T(1024)(128)(4,1)S(1)}, s32[]{:S(2)}) async-start(s8[7962624]{0:T(1024)(128)(4,1)} %bitcast.148), calls=%async_computation.2 | async-start | bytes 8388608
Sparse Core Ops, SparseCore 0:
  12.6 75.1 all-gather.1
where the time goes:
time: 146 us
  waiting for transfers between devices  90.4 us (62%)
  matrix products  21.9 us (15%)
  between operations  14.4 us (10%)
  other arithmetic  9.18 us (6%)
  starting transfers between devices  8.25 us (6%)
  local copies, waits for them, and re-layouts  1.85 us (1%)
    all_gather x1, waiting for transfers between devices, on_device(): portion = lax.all_gather(outgoing, 'tile', axis=1, tiled=True)  73.9 us
    dot_general x27, matrix products, on_device(): jnp.dot(shifted.reshape(-1, channels), w_conv[t_tap, r_tap, c_tap], prefe...  13.3 us
    ppermute x1, waiting for transfers between devices, from_behind(): return lax.ppermute(block, axis, route)  8.22 us
    ppermute x1, starting transfers between devices, extended(): before = lax.ppermute(last, axis, up)  4.37 us
    ppermute x1, waiting for transfers between devices, extended(): before = lax.ppermute(last, axis, up)  4.36 us
    ppermute x1, waiting for transfers between devices, extended(): after = lax.ppermute(first, axis, down)  3.87 us
    select_n x2, other arithmetic, on_device(): jnp.where(usable[:, None, None, None], shifted, jnp.zeros((), shifted.dty...  2.92 us
  transfers between devices with their start and end apart: 4, of which 4 were waited for; matrix products, arithmetic and copies ran while one was open for 1% of the time, Pallas kernels for 0%

commit v1 on v0

--- a/solution.py
+++ b/solution.py
@@ -47,7 +47,35 @@
     score_scale = channels ** (-0.5)
     outgoing = jnp.dot(normed.reshape(-1, channels), kv_weight, preferred_element_type=jnp.float32)
     outgoing = outgoing.astype(jnp.bfloat16).reshape(view_frames, view_cells, 2 * channels)
-    portion = lax.all_gather(outgoing, "tile", axis=1, tiled=True)
+
+    def settle_the_cubes(w_in, pos_dim):
+        block_out, block_last, wide_out = (
+            jax.lax.psum(1, "tile"),
+            jax.lax.axis_index("tile"),
+            w_in.shape[pos_dim],
+        )
+        rack = [to_i * block_out if m == pos_dim else to_i for m, to_i in enumerate(w_in.shape)]
+        res = lax.dynamic_update_slice_in_dim(
+            jnp.zeros(rack, w_in.dtype), w_in, block_last * wide_out, axis=pos_dim
+        )
+        q_next = shaped = w_in
+        for ix in range(1, block_out // 2 + 1):
+            q_next = jax.lax.ppermute(
+                q_next, "tile", list(map(lambda m: (m, (m + 1) % block_out), range(block_out)))
+            )
+            res = lax.dynamic_update_slice_in_dim(
+                res, q_next, (block_last - ix) % block_out * wide_out, axis=pos_dim
+            )
+            if 2 * ix < block_out:
+                shaped = jax.lax.ppermute(
+                    shaped, "tile", list(map(lambda m: (m, (m - 1) % block_out), range(block_out)))
+                )
+                res = lax.dynamic_update_slice_in_dim(
+                    res, shaped, (block_last + ix) % block_out * wide_out, axis=pos_dim
+                )
+        return res
+
+    portion = settle_the_cubes(outgoing, 1)
     key_part = portion[:, :, :channels]
     value_part = portion[:, :, channels:]
     row_top = jnp.full((view_frames, view_cells, 1), -1e30, jnp.float32)

time: 146 us -> 120 us (0.82)
  waiting for transfers between devices: 90.4 us -> 56.1 us
  starting transfers between devices: 8.25 us -> 30.3 us
  between operations: 14.4 us -> 1.09 us
  local copies, waits for them, and re-layouts: 1.85 us -> 4.79 us
  matrix products: 21.9 us -> 19.3 us
    all_gather x1 -> x0, waiting for transfers between devices: 73.9 us -> none  [on_device(): portion = lax.all_gather(outgoing, 'tile', axis=1, tiled=True)]
    ppermute x0 -> x3, waiting for transfers between devices: none -> 40.2 us  [the longest x2 40.2 us: settle_the_cubes(): jax.lax.ppermute(q_next, 'tile', list(map(lambda m: (m, (m + 1) % block_o...]
    ppermute x0 -> x3, starting transfers between devices: none -> 22.5 us  [the longest x2 22 us: settle_the_cubes(): jax.lax.ppermute(q_next, 'tile', list(map(lambda m: (m, (m + 1) % block_o...]
    dynamic_update_slice x0 -> x4, local copies, waits for them, and re-layouts: none -> 2.74 us  [the longest x2 1.36 us: settle_the_cubes(): lax.dynamic_update_slice_in_dim(res, q_next, (block_last - ix) % block_ou...]
    dot_general x1, matrix products: 2.83 us -> 1.16 us  [on_device(): jnp.einsum('fqc,fkc->fqk', queries, key_part, preferred_element_type=jnp....]
  transfers between devices with their start and end apart: 4 -> 6, of which waited for: 4 -> 5; matrix products, arithmetic and copies ran while one was open for 1% -> 3% of each run, Pallas kernels for 0% -> 0%
where the time goes in v1:
time: 120 us
  waiting for transfers between devices  56.1 us (47%)
  starting transfers between devices  30.3 us (25%)
  matrix products  19.3 us (16%)
  other arithmetic  8.47 us (7%)
  local copies, waits for them, and re-layouts  4.79 us (4%)
    ppermute x2, waiting for transfers between devices, settle_the_cubes(): jax.lax.ppermute(q_next, 'tile', list(map(lambda m: (m, (m + 1) % block_o...  40.2 us
    ppermute x2, starting transfers between devices, settle_the_cubes(): jax.lax.ppermute(q_next, 'tile', list(map(lambda m: (m, (m + 1) % block_o...  22 us
    dot_general x27, matrix products, on_device(): jnp.dot(shifted.reshape(-1, channels), w_conv[t_tap, r_tap, c_tap], prefe...  13.3 us
    ppermute x1, waiting for transfers between devices, from_behind(): return lax.ppermute(block, axis, route)  8.22 us
    ppermute x1, waiting for transfers between devices, extended(): before = lax.ppermute(last, axis, up)  4.28 us
    ppermute x1, waiting for transfers between devices, extended(): after = lax.ppermute(first, axis, down)  3.45 us
    ppermute x1, starting transfers between devices, extended(): before = lax.ppermute(last, axis, up)  3.44 us
    select_n x2, other arithmetic, on_device(): jnp.where(usable[:, None, None, None], shifted, jnp.zeros((), shifted.dty...  2.98 us
  transfers between devices with their start and end apart: 6, of which 5 were waited for; matrix products, arithmetic and copies ran while one was open for 3% of the time, Pallas kernels for 0%

profile of v1, /device:TPU:10, one launch (start us, length us, event | category | flops | bytes accessed | tf_op | source)
XLA Modules:
  0.0 120.0 jit_solution(3228166128050574945)
XLA Ops:
  0.6 1.3 %multiply_reduce_fusion = f32[2,2,160]{2,1,0:T(2,128)S(1)} fusion(bf16[2,2,160,384]{3,2,1,0:T(8,128)(2,1)} %param.7), kind=kLoop, calls=%fused_computation.66 | loop fusion | flops 736640 | bytes 494080 | tf_op jit(solution)/shard_map/reduce_sum | solution.py:31
  2.0 1.2 %multiply_convert_fusion.1 = bf16[2,2,160,384]{3,2,1,0:T(8,128)(2,1)S(1)} fusion(bf16[2,2,160,384]{3,2,1,0:T(8,128)(2,1)} %param.7, f32[384]{0:T(512)} %param.9, f32[2,2,160]{2,1,0:T(2,128)S(1)} %add_rsqrt_fusion.1), kind=kLoop, calls=%fused_computation.65 | loop fusion | flops 983040 | bytes 987136 | tf_op jit(solution)/shard_map/convert_element_type | solution.py:38
  3.2 1.7 %convolution_convert_fusion = bf16[640,768]{1,0:T(8,128)(2,1)S(1)} fusion(bf16[640,384]{1,0:T(8,128)(2,1)S(1)} %bitcast.152, bf16[384,1152]{1,0:T(8,128)(2,1)} %param.10), kind=kOutput, calls=%fused_computation.18 | convolution fusion | flops 377978880 | bytes 2064384 | tf_op jit(solution)/shard_map/dot_general | solution.py:48
  4.9 1.6 %collective-permute-start = (bf16[2,320,768]{2,1,0:T(8,128)(2,1)S(1)}, bf16[2,320,768]{2,1,0:T(8,128)(2,1)S(1)}, u32[]{:S(2)}, u32[]{:S(2)}) collective-permute-start(bf16[2,320,768]{2,1,0:T(8,128)(2,1)S(1)} %bitcast.180), channel_id=1, source_target_pairs={{0,4},{4,8},{8,12},{12,0},{1,5},{5,9},{9,13},{13,1},{2,6},{6,10},{... | collective-permute-start | bytes 2949128 | tf_op jit(solution)/shard_map/ppermute | solution.py:63
  7.0 22.6 %collective-permute-done = bf16[2,320,768]{2,1,0:T(8,128)(2,1)S(1)} collective-permute-done((bf16[2,320,768]{2,1,0:T(8,128)(2,1)S(1)}, bf16[2,320,768]{2,1,0:T(8,128)(2,1)S(1)}, u32[]{:S(2)}, u32[]{:S(2)}) %collective-permute-start) | collective-permute-done | bytes 983072 | tf_op jit(solution)/shard_map/ppermute | solution.py:63
  29.6 20.4 %collective-permute-start.2 = (bf16[2,320,768]{2,1,0:T(8,128)(2,1)S(1)}, bf16[2,320,768]{2,1,0:T(8,128)(2,1)}, u32[]{:S(2)}, u32[]{:S(2)}) collective-permute-start(bf16[2,320,768]{2,1,0:T(8,128)(2,1)S(1)} %collective-permute-done), channel_id=1, source_target_pairs={{0,4},{4,8},{8,12},{12,0},{1,5},{5,9},{9,13},{13,1},{2,6},{6,10},{... | collective-permute-start | bytes 2949128 | tf_op jit(solution)/shard_map/ppermute | solution.py:63
  50.4 1.4 %convolution_convert_fusion.1 = bf16[640,384]{1,0:T(8,128)(2,1)S(1)} fusion(bf16[640,384]{1,0:T(8,128)(2,1)S(1)} %bitcast.153, bf16[384,1152]{1,0:T(8,128)(2,1)} %param.10), kind=kOutput, calls=%fused_computation.46 | convolution fusion | flops 188989440 | bytes 1277952 | tf_op jit(solution)/shard_map/dot_general | solution.py:42
  51.9 1.3 %constant_dynamic-update-slice_fusion.1 = bf16[2,1280,768]{2,1,0:T(8,128)(2,1)S(1)} fusion(bf16[2,1280,768]{2,1,0:T(8,128)(2,1)S(1)} %constant_dynamic-update-slice_fusion.2, bf16[2,320,768]{2,1,0:T(8,128)(2,1)} %collective-permute-done.1, s32[]{:T(128)S(6)} %select_n.118), kind=kLoop, calls=%fused_computation.166 | loop fusion | bytes 1966084 | tf_op jit(solution)/shard_map/dynamic_update_slice | solution.py:73
  53.2 17.6 %collective-permute-done.2 = bf16[2,320,768]{2,1,0:T(8,128)(2,1)} collective-permute-done((bf16[2,320,768]{2,1,0:T(8,128)(2,1)S(1)}, bf16[2,320,768]{2,1,0:T(8,128)(2,1)}, u32[]{:S(2)}, u32[]{:S(2)}) %collective-permute-start.2) | collective-permute-done | bytes 983072 | tf_op jit(solution)/shard_map/ppermute | solution.py:63
  70.8 1.3 %constant_dynamic-update-slice_fusion = bf16[2,1280,768]{2,1,0:T(8,128)(2,1)S(1)} fusion(bf16[2,1280,768]{2,1,0:T(8,128)(2,1)S(1)} %constant_dynamic-update-slice_fusion.1, bf16[2,320,768]{2,1,0:T(8,128)(2,1)} %collective-permute-done.2, s32[]{:T(128)S(6)} %select_n.120), kind=kLoop, calls=%fused_computation.165 | loop fusion | bytes 1966084 | tf_op jit(solution)/shard_map/dynamic_update_slice | solution.py:66
  72.0 1.2 fusion.98
  73.2 0.6 fusion.1
  73.9 1.1 divide_convert_fusion
  75.0 0.6 fusion.14
  76.0 1.9 %collective-permute-start.3 = (bf16[2,2,160,384]{3,2,1,0:T(8,128)(2,1)S(1)}, bf16[2,2,160,384]{3,2,1,0:T(8,128)(2,1)S(1)}, u32[]{:S(2)}, u32[]{:S(2)}) collective-permute-start(bf16[2,2,160,384]{3,2,1,0:T(8,128)(2,1)S(1)} %multiply_convert_fusion), channel_id=1, source_target_pairs={{0,1},{1,2},{2,3},{4,5},{5,6},{6,7},{8,9},{9,10},{10,11},{12,13},{... | collective-permute-start | bytes 1474568 | tf_op jit(solution)/shard_map/ppermute | solution.py:12
  78.0 8.2 %collective-permute-done.3 = bf16[2,2,160,384]{3,2,1,0:T(8,128)(2,1)S(1)} collective-permute-done((bf16[2,2,160,384]{3,2,1,0:T(8,128)(2,1)S(1)}, bf16[2,2,160,384]{3,2,1,0:T(8,128)(2,1)S(1)}, u32[]{:S(2)}, u32[]{:S(2)}) %collective-permute-start.3) | collective-permute-done | bytes 491552 | tf_op jit(solution)/shard_map/ppermute | solution.py:12
  86.3 3.4 %collective-permute-start.4 = (bf16[4,1,160,384]{3,2,1,0:T(8,128)(2,1)S(1)}, bf16[4,1,160,384]{3,2,1,0:T(8,128)(2,1)S(1)}, u32[]{:S(2)}, u32[]{:S(2)}) collective-permute-start(bf16[4,1,160,384]{3,2,1,0:T(8,128)(2,1)S(1)} %get-tuple-element.34), channel_id=1, source_target_pairs={{0,4},{4,8},{8,12},{1,5},{5,9},{9,13},{2,6},{6,10},{10,14},{3,7},{... | collective-permute-start | bytes 1474568 | tf_op jit(solution)/shard_map/ppermute | solution.py:22
  89.8 2.4 %collective-permute-start.5 = (bf16[4,1,160,384]{3,2,1,0:T(8,128)(2,1)S(1)}, bf16[4,1,160,384]{3,2,1,0:T(8,128)(2,1)S(1)}, u32[]{:S(2)}, u32[]{:S(2)}) collective-permute-start(bf16[4,1,160,384]{3,2,1,0:T(8,128)(2,1)S(1)} %get-tuple-element.35), channel_id=1, source_target_pairs={{4,0},{8,4},{12,8},{5,1},{9,5},{13,9},{6,2},{10,6},{14,10},{7,3},{... | collective-permute-start | bytes 1474568 | tf_op jit(solution)/shard_map/ppermute | solution.py:23
  92.7 4.3 %collective-permute-done.4 = bf16[4,1,160,384]{3,2,1,0:T(8,128)(2,1)S(1)} collective-permute-done((bf16[4,1,160,384]{3,2,1,0:T(8,128)(2,1)S(1)}, bf16[4,1,160,384]{3,2,1,0:T(8,128)(2,1)S(1)}, u32[]{:S(2)}, u32[]{:S(2)}) %collective-permute-start.4) | collective-permute-done | bytes 491552 | tf_op jit(solution)/shard_map/ppermute | solution.py:22
  97.0 3.4 %collective-permute-done.5 = bf16[4,1,160,384]{3,2,1,0:T(8,128)(2,1)S(1)} collective-permute-done((bf16[4,1,160,384]{3,2,1,0:T(8,128)(2,1)S(1)}, bf16[4,1,160,384]{3,2,1,0:T(8,128)(2,1)S(1)}, u32[]{:S(2)}, u32[]{:S(2)}) %collective-permute-start.5) | collective-permute-done | bytes 491552 | tf_op jit(solution)/shard_map/ppermute | solution.py:23
  100.5 1.2 select_maximum_fusion
  101.7 1.4 %slice_select_fusion = (bf16[2,2,160,384]{3,2,1,0:T(8,128)(2,1)S(1)}, bf16[2,2,160,384]{3,2,1,0:T(8,128)(2,1)S(1)}, bf16[2,2,160,384]{3,2,1,0:T(8,128)(2,1)S(1)}...) fusion(bf16[4,4,162,384]{3,2,1,0:T(8,128)(2,1)S(1)} %select_max, ...), kind=kLoop, calls=%fused_computation.71 | loop fusion | flops 2949120 | bytes 11796484 | tf_op jit(solution)/shard_map/jit(_where)/select_n | solution.py:119
  103.4 1.6 %slice_select_fusion.6 = (bf16[2,2,160,384]{3,2,1,0:T(8,128)(2,1)S(1)}, bf16[2,2,160,384]{3,2,1,0:T(8,128)(2,1)S(1)}, bf16[2,2,160,384]{3,2,1,0:T(8,128)(2,1)S(1...) fusion(bf16[4,3,160,384]{3,2,1,0:T(8,128)(2,1)S(1)} %get-tuple-, ...), kind=kLoop, calls=%fused_computation.77 | loop fusion | flops 3686400 | bytes 13762566 | tf_op jit(solution)/shard_map/jit(_where)/select_n | solution.py:119
  105.1 1.3 %slice-done.1 = s8[4194304]{0:T(1024)(128)(4,1)S(1)} async-done(((s8[7962624]{0:T(1024)(128)(4,1)}), s8[4194304]{0:T(1024)(128)(4,1)S(1)}, s32[]{:S(2)}) %slice-start.1) | async-done | bytes 4194328
  107.4 0.5 convolution_add_fusion.24
  107.9 0.5 convolution_add_fusion.23
  108.3 0.5 convolution_add_fusion.22
  109.3 0.5 convolution_add_fusion.20
  116.2 0.5 convolution_add_fusion.5
  116.7 0.6 convolution_add_fusion.4
  118.3 0.5 convolution_add_fusion.1
  118.8 1.2 %fusion.13 = bf16[640,384]{1,0:T(8,128)(2,1)} fusion(f32[640,384]{1,0:T(8,128)S(1)} %convolution_add_fusion.1, bf16[640,384]{1,0:T(8,128)(2,1)S(1)} %bitcast.154, bf16[3,3,3,384,384]{4,3,2,1,0:T(8,128)(2,1)S(1)} %bitcast.149), kind=kOutput, calls=%fused_computation.48 | convolution fusion | flops 189235200 | bytes 2260992 | tf_op jit(solution)/shard_map/dot_general | solution.py:122
  (53 shorter events, 11.1 us)
Async XLA Ops:
  0.6 74.4 %copy-start = (bf16[384,384]{1,0:T(8,128)(2,1)S(1)}, bf16[384,384]{1,0:T(8,128)(2,1)}, u32[]{:S(2)}) copy-start(bf16[384,384]{1,0:T(8,128)(2,1)} %param.11) | copy-start | bytes 884740
  4.9 24.7 %collective-permute-start = (bf16[2,320,768]{2,1,0:T(8,128)(2,1)S(1)}, bf16[2,320,768]{2,1,0:T(8,128)(2,1)S(1)}, u32[]{:S(2)}, u32[]{:S(2)}) collective-permute-start(bf16[2,320,768]{2,1,0:T(8,128)(2,1)S(1)} %bitcast.180), channel_id=1, source_target_pairs={{0,4},{4,8},{8,12},{12,0},{1,5},{5,9},{9,13},{13,1},{2,6},{6,10},{... | collective-permute-start | bytes 2949128 | tf_op jit(solution)/shard_map/ppermute | solution.py:63
  6.6 45.3 %collective-permute-start.1 = (bf16[2,320,768]{2,1,0:T(8,128)(2,1)S(1)}, bf16[2,320,768]{2,1,0:T(8,128)(2,1)}, u32[]{:S(2)}, u32[]{:S(2)}) collective-permute-start(bf16[2,320,768]{2,1,0:T(8,128)(2,1)S(1)} %bitcast.181), channel_id=1, source_target_pairs={{0,12},{4,0},{8,4},{12,8},{1,13},{5,1},{9,5},{13,9},{2,14},{6,2},{... | collective-permute-start | bytes 2949128 | tf_op jit(solution)/shard_map/ppermute | solution.py:70
  29.6 41.1 %collective-permute-start.2 = (bf16[2,320,768]{2,1,0:T(8,128)(2,1)S(1)}, bf16[2,320,768]{2,1,0:T(8,128)(2,1)}, u32[]{:S(2)}, u32[]{:S(2)}) collective-permute-start(bf16[2,320,768]{2,1,0:T(8,128)(2,1)S(1)} %collective-permute-done), channel_id=1, source_target_pairs={{0,4},{4,8},{8,12},{12,0},{1,5},{5,9},{9,13},{13,1},{2,6},{6,10},{... | collective-permute-start | bytes 2949128 | tf_op jit(solution)/shard_map/ppermute | solution.py:63
  73.9 1.1 copy-start.2
  73.9 1.8 %copy-start.4 = (f32[384]{0:T(512)S(1)}, f32[384]{0:T(512)}, u32[]{:S(2)}) copy-start(f32[384]{0:T(512)} %param.12) | copy-start | bytes 4612
  75.0 17.2 %copy-start.5 = (s32[4]{0:T(128)S(1)}, s32[4]{0:T(128)}, u32[]{:S(2)}) copy-start(s32[4]{0:T(128)} %param.8) | copy-start | bytes 52
  75.6 41.1 %copy-start.3 = (bf16[640,384]{1,0:T(8,128)(2,1)}, bf16[640,384]{1,0:T(8,128)(2,1)S(1)}, u32[]{:S(2)}) copy-start(bf16[640,384]{1,0:T(8,128)(2,1)S(1)} %get-tuple-element.55) | copy-start | bytes 1474564
  76.0 10.1 %collective-permute-start.3 = (bf16[2,2,160,384]{3,2,1,0:T(8,128)(2,1)S(1)}, bf16[2,2,160,384]{3,2,1,0:T(8,128)(2,1)S(1)}, u32[]{:S(2)}, u32[]{:S(2)}) collective-permute-start(bf16[2,2,160,384]{3,2,1,0:T(8,128)(2,1)S(1)} %multiply_convert_fusion), channel_id=1, source_target_pairs={{0,1},{1,2},{2,3},{4,5},{5,6},{6,7},{8,9},{9,10},{10,11},{12,13},{... | collective-permute-start | bytes 1474568 | tf_op jit(solution)/shard_map/ppermute | solution.py:12
  86.3 10.7 %collective-permute-start.4 = (bf16[4,1,160,384]{3,2,1,0:T(8,128)(2,1)S(1)}, bf16[4,1,160,384]{3,2,1,0:T(8,128)(2,1)S(1)}, u32[]{:S(2)}, u32[]{:S(2)}) collective-permute-start(bf16[4,1,160,384]{3,2,1,0:T(8,128)(2,1)S(1)} %get-tuple-element.34), channel_id=1, source_target_pairs={{0,4},{4,8},{8,12},{1,5},{5,9},{9,13},{2,6},{6,10},{10,14},{3,7},{... | collective-permute-start | bytes 1474568 | tf_op jit(solution)/shard_map/ppermute | solution.py:22
  89.8 10.7 %collective-permute-start.5 = (bf16[4,1,160,384]{3,2,1,0:T(8,128)(2,1)S(1)}, bf16[4,1,160,384]{3,2,1,0:T(8,128)(2,1)S(1)}, u32[]{:S(2)}, u32[]{:S(2)}) collective-permute-start(bf16[4,1,160,384]{3,2,1,0:T(8,128)(2,1)S(1)} %get-tuple-element.35), channel_id=1, source_target_pairs={{4,0},{8,4},{12,8},{5,1},{9,5},{13,9},{6,2},{10,6},{14,10},{7,3},{... | collective-permute-start | bytes 1474568 | tf_op jit(solution)/shard_map/ppermute | solution.py:23
  103.1 2.1 %slice-start = ((s8[7962624]{0:T(1024)(128)(4,1)}), s8[3768320]{0:T(1024)(128)(4,1)S(1)}, s32[]{:S(2)}) async-start(s8[7962624]{0:T(1024)(128)(4,1)} %bitcast.148), calls=%async_computation | async-start | bytes 7536640
  103.4 3.1 %slice-start.1 = ((s8[7962624]{0:T(1024)(128)(4,1)}), s8[4194304]{0:T(1024)(128)(4,1)S(1)}, s32[]{:S(2)}) async-start(s8[7962624]{0:T(1024)(128)(4,1)} %bitcast.148), calls=%async_computation.1 | async-start | bytes 8388608
  117.4 2.7 %copy-start.1 = (bf16[384,384]{1,0:T(8,128)(2,1)S(1)}, bf16[384,384]{1,0:T(8,128)(2,1)}, u32[]{:S(2)}) copy-start(bf16[384,384]{1,0:T(8,128)(2,1)} %param.11) | copy-start | bytes 884740
